TPU v7x, 256 devices: a whole 4x4x8 slice. The times are simulated.
256 devices in a mesh: sta: 8 (over x, y_lo), tm: 32 (over z, y_hi, core).
Axes of the slice: x: 4, y: 4 (y_hi: 2, y_lo: 2; y = y_hi * 2 + y_lo), z: 8, core: 2. Of those that a mesh axis runs over, the one named last changes fastest.
Arguments:
- record: bfloat16 [16, 3, 16384], P('sta', None, 'tm'), may hold values from -6 to 6
- templates: bfloat16 [16, 256, 768], P('sta'), may hold values from -6 to 6
- moveouts: int32 [16, 256], P('sta'), may hold values from 0 to 255
- live_mask: int32 [16], P('sta'), may hold values 0 or 1
- owner_order: int32 [256], replicated, may hold values from 0 to 255, each once
Outputs:
- detection: float32 [256, 16384], P('sta', 'tm')
All inputs are finite; a program needn't handle non-finite values. No bound on the sum of `live_mask` on one device may be relied on, other than what follows from the above.
Results may differ from a plain program's by a relative error of at most 0.0029.
Values may be sent and summed in bfloat16 or wider, within the bound.
No kernel may reach another device: no remote copies, remote signals or barrier semaphores. Data moves between devices by JAX's collectives and lax.ppermute only.
A program may use at most 64 MiB of HBM per device.

v0:
```python
import math
import jax
import jax.numpy as jnp
from jax import lax
from jax.sharding import PartitionSpec as P

TLEN = 256
MAXM = 256
epsilon = 1e-05


def passed_along(value, axis, steps):
    count = lax.axis_size(axis)
    initial, last = (max(0, -steps), min(count, count - steps))
    return lax.ppermute(value, axis, [(source, source + steps) for source in range(initial, last)])


def toeplitz(signal, span, width):
    components = signal.shape[0]
    length = width + span
    tiled = jnp.tile(signal, (1, span + 1))
    flat = tiled[:, : span * (length + 1)]
    return flat.reshape(components, span, length + 1)[:, :, :width]


def normalize_block(extended, templates, columns):
    components = extended.shape[1]

    def one_station(items):
        record_one, template_one = items
        squares = jnp.sum(jnp.square(record_one.astype(jnp.float32)), axis=0)
        running = jnp.concatenate([jnp.zeros((1,), jnp.float32), jnp.cumsum(squares)])
        energy = running[TLEN : TLEN + columns] - running[:columns]
        record_rms = jnp.sqrt(energy / (components * TLEN) + epsilon)
        template_rms = jnp.sqrt(
            jnp.mean(jnp.square(template_one.astype(jnp.float32)), axis=-1) + epsilon
        )
        frames = toeplitz(record_one, TLEN, columns).reshape(components * TLEN, columns)
        correlation = jnp.dot(template_one, frames, preferred_element_type=jnp.float32)
        scaled = correlation / (components * TLEN * record_rms[None, :] * template_rms[:, None])
        return scaled.astype(jnp.bfloat16)

    return lax.map(one_station, (extended, templates))


def shift_rows(values, shifts, width):
    current = values
    for bit_place in reversed(range((MAXM - 1).bit_length())):
        step_size = 1 << bit_place
        new_len = current.shape[-1] - step_size
        taken = shifts >> bit_place & 1 == 1
        current = jnp.where(
            taken[..., None], current[..., step_size : step_size + new_len], current[..., :new_len]
        )
    return current[..., :width]


def shards(record, templates, moveouts, live_mask, owner_order):
    stations = record.shape[0]
    components = record.shape[1]
    block_len = record.shape[2]
    kcount = templates.shape[1]
    next_rim = passed_along(record[:, :, :TLEN], "tm", -1)
    extended = jnp.concatenate([record, next_rim], axis=2)
    own_scores = normalize_block(extended, templates, block_len)
    borrowed = passed_along(own_scores[:, :, :MAXM], "tm", -1)
    scores = jnp.concatenate([own_scores, borrowed], axis=2)
    stack_scale = math.sqrt(components * TLEN / (stations * lax.axis_size("sta")))
    weights = live_mask.astype(jnp.float32) * stack_scale
    own_rows = kcount // lax.axis_size("sta")
    chosen_scores = jnp.take(scores, owner_order, axis=1)
    shifts = jnp.take(moveouts, owner_order, axis=1)
    picked = shift_rows(chosen_scores, shifts, block_len)
    summed = lax.psum(jnp.sum(picked.astype(jnp.float32) * weights[:, None, None], axis=0), "sta")
    return lax.dynamic_slice_in_dim(summed, lax.axis_index("sta") * own_rows, own_rows, 0)


def solution(mesh):
    placed = (P("sta", None, "tm"), P("sta", None, None), P("sta", None), P("sta"), P())
    return jax.shard_map(
        shards, mesh=mesh, in_specs=placed, out_specs=P("sta", "tm"), check_vma=False
    )
```

profile of v0, /device:TPU:32, one launch (start us, length us, event | category | flops | bytes accessed | tf_op | source)
XLA Modules:
  0.0 152.0 jit_solution(10830028386999631244)
XLA Ops:
  6.5 0.7 copy.33
  7.2 4.1 %collective-permute-start = (bf16[2,3,256]{2,1,0:T(4,128)(2,1)S(1)}, bf16[2,3,256]{2,1,0:T(4,128)(2,1)S(1)}, u32[]{:S(2)}, u32[]{:S(2)}) collective-permute-start(bf16[2,3,256]{2,1,0:T(4,128)(2,1)S(1)} %slice.101), channel_id=1, source_target_pairs={{1,0},{2,1},{3,2},{4,3},{5,4},{6,5},{7,6},{8,7},{9,8},{10,9},{11,1... | collective-permute-start | bytes 9224 | tf_op jit(solution)/shard_map/ppermute | solution.py:15
  11.3 0.7 compare_select_fusion
  12.0 0.7 compare_and_fusion
  12.7 0.8 copy.22
  13.5 0.7 gather_fusion
  14.4 16.3 %while.10 = (s32[]{:T(128)}, bf16[2,256,512]{2,1,0:T(8,128)(2,1)}, bf16[2,256,768]{2,1,0:T(8,128)(2,1)}, bf16[2,3,768]{2,1,0:T(4,128)(2,1)S(1)}, s32[]{:T(128)}, /*index=5*/f32[]{:T(128)}, f32[1]{0:T(128)}) while((s32[]{:T(128)}, bf16[2,256,512]{2,1,0:T(8,128)(2,1)}, bf16[2,256,768]{2,1,0:T(8,128)(2,1)}, bf16[2,3,768]{2,1,0:T(4,128)(2,1)S(1)}, ...), condition=%wide.region_5.6_spmd, body=%wide.region_0.5_spmd.sunk | while | flops 202417184 | bytes 21436772 | solution.py:43
  16.5 1.0 reshape.175
  17.5 2.8 %reshape.176 = bf16[3,256,769]{2,1,0:T(8,128)(2,1)S(1)} reshape(bf16[590592]{0:T(1024)(128)(2,1)S(1)} %reshape.175) | data formatting | bytes 2362368 | tf_op jit(solution)/shard_map/while/body/eval_jaxpr/reshape | solution.py:23
  20.6 0.8 copy-done.1
  21.7 0.8 copy-done.2
  24.6 1.0 reshape.175
  25.6 2.8 %reshape.176 = bf16[3,256,769]{2,1,0:T(8,128)(2,1)S(1)} reshape(bf16[590592]{0:T(1024)(128)(2,1)S(1)} %reshape.175) | data formatting | bytes 2362368 | tf_op jit(solution)/shard_map/while/body/eval_jaxpr/reshape | solution.py:23
  28.7 0.8 copy-done.1
  29.9 0.8 copy-done.2
  30.7 1.6 %copy.35 = bf16[2,256,512]{2,0,1:T(2,128)(2,1)S(1)} copy(bf16[2,256,512]{2,1,0:T(8,128)(2,1)} %get-tuple-element.27) | data formatting | bytes 1048576 | tf_op jit(solution)/shard_map/while | solution.py:43
  32.4 4.5 %collective-permute-start.1 = (bf16[2,256,256]{2,0,1:T(2,128)(2,1)S(1)}, bf16[2,256,256]{2,0,1:T(2,128)(2,1)S(1)}, u32[]{:S(2)}, u32[]{:S(2)}) collective-permute-start(bf16[2,256,256]{2,0,1:T(2,128)(2,1)S(1)} %slice.102), channel_id=1, source_target_pairs={{1,0},{2,1},{3,2},{4,3},{5,4},{6,5},{7,6},{8,7},{9,8},{10,9},{11,1... | collective-permute-start | bytes 786440 | tf_op jit(solution)/shard_map/ppermute | solution.py:15
  38.4 2.2 %collective-permute-done.1 = bf16[2,256,256]{2,0,1:T(2,128)(2,1)S(1)} collective-permute-done((bf16[2,256,256]{2,0,1:T(2,128)(2,1)S(1)}, bf16[2,256,256]{2,0,1:T(2,128)(2,1)S(1)}, u32[]{:S(2)}, u32[]{:S(2)}) %collective-permute-start.1) | collective-permute-done | bytes 262176 | tf_op jit(solution)/shard_map/ppermute | solution.py:15
  40.6 0.7 pad_maximum_fusion.1
  41.3 2.3 %gather_fusion.1 = bf16[256,2,768]{2,1,0:T(2,128)(2,1)S(1)} fusion(bf16[2,256,768]{2,0,1:T(2,128)(2,1)S(1)} %pad_maximum_fusion.1, s32[1024]{0:T(1024)S(1)} %pad_clamp_fusion), kind=kCustom, calls=%fused_computation.1 | custom fusion | bytes 1573888 | tf_op jit(solution)/shard_map/jit(_take)/gather | solution.py:71
  43.6 1.3 fusion.6
  44.9 1.1 broadcast_select_fusion.1
  46.0 1.5 broadcast_select_fusion.2
  47.5 1.5 broadcast_select_fusion.3
  49.0 1.5 broadcast_select_fusion.4
  50.5 1.5 broadcast_select_fusion.5
  52.0 1.5 broadcast_select_fusion.6
  53.6 1.5 broadcast_select_fusion.7
  55.1 1.7 %fusion.7 = (bf16[2,256,513]{2,0,1:T(2,128)(2,1)S(1)}, bf16[2,256,513]{2,0,1:T(2,128)(2,1)S(1)}) fusion(bf16[2,256,514]{2,0,1:T(2,128)(2,1)S(1)} %broadcast_select_fusion.7), kind=kLoop, calls=%fused_computation.45 | loop fusion | bytes 2101248 | tf_op jit(solution)/shard_map/slice | solution.py:53
  56.8 2.7 %multiply_reduce_fusion.2 = f32[256,512]{1,0:T(8,128)} fusion(f32[2]{0:T(128)S(1)} %convert_multiply_fusion, pred[2,256]{0,1:T(8,128)(4,1)S(1)} %copy.24, bf16[2,256,513]{2,0,1:T(2,128)(2,1)S(1)} %get-tuple-element.39, bf16[2,256,513]{2,0,1:T(2,128)(2,1)S(1)} %get-tuple-element.38), kind=kLoop, calls=%fused_computation.26 | loop fusion | flops 917504 | bytes 1573384 | tf_op jit(solution)/shard_map/reduce_sum | solution.py:74
  59.5 84.2 %all-reduce.2.cloned.1.call-done = f32[256,512]{1,0:T(8,128)} async-done(((f32[256,512]{1,0:T(8,128)}), f32[256,512]{1,0:T(8,128)}) %all-reduce.2.cloned.1.call-update) | async-done | bytes 524304 | tf_op jit(solution)/shard_map/psum | solution.py:74
  143.7 1.5 constant_dynamic-slice_fusion
  (59 shorter events, 7.1 us)
Async XLA Ops:
  6.5 137.1 %all-reduce.2.cloned.1.call-start = ((), (), s32[]{:S(2)}) async-start(), calls=%async_computation | async-start | bytes 1048576 | tf_op jit(solution)/shard_map/psum | solution.py:74
  7.2 7.1 %collective-permute-start = (bf16[2,3,256]{2,1,0:T(4,128)(2,1)S(1)}, bf16[2,3,256]{2,1,0:T(4,128)(2,1)S(1)}, u32[]{:S(2)}, u32[]{:S(2)}) collective-permute-start(bf16[2,3,256]{2,1,0:T(4,128)(2,1)S(1)} %slice.101), channel_id=1, source_target_pairs={{1,0},{2,1},{3,2},{4,3},{5,4},{6,5},{7,6},{8,7},{9,8},{10,9},{11,1... | collective-permute-start | bytes 9224 | tf_op jit(solution)/shard_map/ppermute | solution.py:15
  17.5 2.9 %copy-start = (bf16[2,256,768]{2,1,0:T(8,128)(2,1)S(1)}, bf16[2,256,768]{2,1,0:T(8,128)(2,1)}, u32[]{:S(2)}) copy-start(bf16[2,256,768]{2,1,0:T(8,128)(2,1)} %get-tuple-element.93) | copy-start | bytes 2359300 | tf_op jit(solution)/shard_map/while
  20.3 1.0 copy-start.1
  21.7 0.8 copy-start.2
  25.6 2.9 %copy-start = (bf16[2,256,768]{2,1,0:T(8,128)(2,1)S(1)}, bf16[2,256,768]{2,1,0:T(8,128)(2,1)}, u32[]{:S(2)}) copy-start(bf16[2,256,768]{2,1,0:T(8,128)(2,1)} %get-tuple-element.93) | copy-start | bytes 2359300 | tf_op jit(solution)/shard_map/while
  28.4 1.0 copy-start.1
  29.9 0.8 copy-start.2
  30.7 7.8 %copy-start.3 = (s32[2]{0:T(128)S(1)}, s32[2]{0:T(128)}, u32[]{:S(2)}) copy-start(s32[2]{0:T(128)} %param.10) | copy-start | bytes 28
  32.4 8.2 %collective-permute-start.1 = (bf16[2,256,256]{2,0,1:T(2,128)(2,1)S(1)}, bf16[2,256,256]{2,0,1:T(2,128)(2,1)S(1)}, u32[]{:S(2)}, u32[]{:S(2)}) collective-permute-start(bf16[2,256,256]{2,0,1:T(2,128)(2,1)S(1)} %slice.102), channel_id=1, source_target_pairs={{1,0},{2,1},{3,2},{4,3},{5,4},{6,5},{7,6},{8,7},{9,8},{10,9},{11,1... | collective-permute-start | bytes 786440 | tf_op jit(solution)/shard_map/ppermute | solution.py:15
Sparse Core Ops, SparseCore 0:
  59.6 84.0 all-reduce.1
where the time goes:
time: 152 us
  waiting for transfers between devices  86.4 us (57%)
  local copies, waits for them, and re-layouts  24.9 us (16%)
  other arithmetic  17.7 us (12%)
  between operations  13.6 us (9%)
  starting transfers between devices  8.56 us (6%)
    psum x1, waiting for transfers between devices, shards(): lax.psum(jnp.sum(picked.astype(jnp.float32) * weights[:, None, None], axi...  84.2 us
    select_n x7, other arithmetic, shift_rows(): jnp.where(taken[..., None], current[..., step_size:step_size + new_len],...  10.1 us
    ppermute x2, starting transfers between devices, passed_along(): lax.ppermute(value, axis, [(source, source + steps) for source in range(i...  8.56 us
    while x18, local copies, waits for them, and re-layouts  6.53 us
    reshape x2, local copies, waits for them, and re-layouts, toeplitz(): return flat.reshape(components, span, length + 1)[:, :, :width]  5.62 us
  transfers between devices with their start and end apart: 3, of which 2 were waited for; matrix products, arithmetic and copies ran while one was open for 3% of the time, Pallas kernels for 0%

commit v1 on v0

--- a/solution.py
+++ b/solution.py
@@ -71,7 +71,10 @@
     chosen_scores = jnp.take(scores, owner_order, axis=1)
     shifts = jnp.take(moveouts, owner_order, axis=1)
     picked = shift_rows(chosen_scores, shifts, block_len)
-    summed = lax.psum(jnp.sum(picked.astype(jnp.float32) * weights[:, None, None], axis=0), "sta")
+    summed = jnp.sum(
+        lax.all_gather(jnp.sum(picked.astype(jnp.float32) * weights[:, None, None], axis=0), "sta"),
+        axis=0,
+    )
     return lax.dynamic_slice_in_dim(summed, lax.axis_index("sta") * own_rows, own_rows, 0)
 
 

time: 152 us -> 169 us (1.11); the launches traced: 152 us -> 166 us
  waiting for transfers between devices: 86.4 us -> 99 us
  other arithmetic: 17.7 us -> 20.5 us
    all_gather x0 -> x1, waiting for transfers between devices: none -> 96.7 us  [shards(): lax.all_gather(jnp.sum(picked.astype(jnp.float32) * weights[:, None, None...]
    psum x1 -> x0, waiting for transfers between devices: 84.2 us -> none  [shards(): lax.psum(jnp.sum(picked.astype(jnp.float32) * weights[:, None, None], axi...]
    reduce_sum x0 -> x1, other arithmetic: none -> 2.7 us  [shards(): jnp.sum(lax.all_gather(jnp.sum(picked.astype(jnp.float32) * weights[:, No...]
where the time goes in v1:
time: 169 us; the launch traced here: 166 us
  waiting for transfers between devices  99 us (59%)
  local copies, waits for them, and re-layouts  24 us (14%)
  other arithmetic  20.5 us (12%)
  between operations  13.6 us (8%)
  starting transfers between devices  8.38 us (5%)
    all_gather x1, waiting for transfers between devices, shards(): lax.all_gather(jnp.sum(picked.astype(jnp.float32) * weights[:, None, None...  96.7 us
    select_n x7, other arithmetic, shift_rows(): jnp.where(taken[..., None], current[..., step_size:step_size + new_len],...  10.1 us
    ppermute x2, starting transfers between devices, passed_along(): lax.ppermute(value, axis, [(source, source + steps) for source in range(i...  8.38 us
    while x18, local copies, waits for them, and re-layouts  6.53 us
    reshape x2, local copies, waits for them, and re-layouts, toeplitz(): return flat.reshape(components, span, length + 1)[:, :, :width]  5.62 us
  transfers between devices with their start and end apart: 3, of which 2 were waited for; matrix products, arithmetic and copies ran while one was open for 3% of the time, Pallas kernels for 0%

profile of v1, /device:TPU:32, one launch (start us, length us, event | category | flops | bytes accessed | tf_op | source)
XLA Modules:
  0.0 166.5 jit_solution(9600956445795321721)
XLA Ops:
  6.5 0.7 copy.38
  7.2 4.1 %collective-permute-start = (bf16[2,3,256]{2,1,0:T(4,128)(2,1)S(1)}, bf16[2,3,256]{2,1,0:T(4,128)(2,1)S(1)}, u32[]{:S(2)}, u32[]{:S(2)}) collective-permute-start(bf16[2,3,256]{2,1,0:T(4,128)(2,1)S(1)} %slice.101), channel_id=1, source_target_pairs={{1,0},{2,1},{3,2},{4,3},{5,4},{6,5},{7,6},{8,7},{9,8},{10,9},{11,1... | collective-permute-start | bytes 9224 | tf_op jit(solution)/shard_map/ppermute | solution.py:15
  11.3 0.7 compare_select_fusion
  12.0 0.7 compare_and_fusion
  12.7 0.8 copy.27
  13.5 0.7 gather_fusion
  14.4 16.3 %while.10 = (s32[]{:T(128)}, bf16[2,256,512]{2,1,0:T(8,128)(2,1)}, bf16[2,256,768]{2,1,0:T(8,128)(2,1)}, bf16[2,3,768]{2,1,0:T(4,128)(2,1)S(1)}, s32[]{:T(128)}, /*index=5*/f32[]{:T(128)}, f32[1]{0:T(128)}) while((s32[]{:T(128)}, bf16[2,256,512]{2,1,0:T(8,128)(2,1)}, bf16[2,256,768]{2,1,0:T(8,128)(2,1)}, bf16[2,3,768]{2,1,0:T(4,128)(2,1)S(1)}, ...), condition=%wide.region_5.6_spmd, body=%wide.region_0.5_spmd.sunk | while | flops 202417184 | bytes 21436772 | solution.py:43
  16.5 1.0 reshape.176
  17.5 2.8 %reshape.177 = bf16[3,256,769]{2,1,0:T(8,128)(2,1)S(1)} reshape(bf16[590592]{0:T(1024)(128)(2,1)S(1)} %reshape.176) | data formatting | bytes 2362368 | tf_op jit(solution)/shard_map/while/body/eval_jaxpr/reshape | solution.py:23
  20.6 0.8 copy-done.1
  21.7 0.8 copy-done.2
  24.6 1.0 reshape.176
  25.6 2.8 %reshape.177 = bf16[3,256,769]{2,1,0:T(8,128)(2,1)S(1)} reshape(bf16[590592]{0:T(1024)(128)(2,1)S(1)} %reshape.176) | data formatting | bytes 2362368 | tf_op jit(solution)/shard_map/while/body/eval_jaxpr/reshape | solution.py:23
  28.7 0.8 copy-done.1
  29.9 0.8 copy-done.2
  30.7 1.6 copy.40
  32.4 4.3 %collective-permute-start.1 = (bf16[2,256,256]{2,0,1:T(2,128)(2,1)S(1)}, bf16[2,256,256]{2,0,1:T(2,128)(2,1)S(1)}, u32[]{:S(2)}, u32[]{:S(2)}) collective-permute-start(bf16[2,256,256]{2,0,1:T(2,128)(2,1)S(1)} %slice.102), channel_id=1, source_target_pairs={{1,0},{2,1},{3,2},{4,3},{5,4},{6,5},{7,6},{8,7},{9,8},{10,9},{11,1... | collective-permute-start | bytes 786440 | tf_op jit(solution)/shard_map/ppermute | solution.py:15
  38.3 2.3 %collective-permute-done.1 = bf16[2,256,256]{2,0,1:T(2,128)(2,1)S(1)} collective-permute-done((bf16[2,256,256]{2,0,1:T(2,128)(2,1)S(1)}, bf16[2,256,256]{2,0,1:T(2,128)(2,1)S(1)}, u32[]{:S(2)}, u32[]{:S(2)}) %collective-permute-start.1) | collective-permute-done | bytes 262176 | tf_op jit(solution)/shard_map/ppermute | solution.py:15
  40.6 0.7 pad_maximum_fusion.1
  41.3 2.3 %gather_fusion.1 = bf16[256,2,768]{2,1,0:T(2,128)(2,1)S(1)} fusion(bf16[2,256,768]{2,0,1:T(2,128)(2,1)S(1)} %pad_maximum_fusion.1, s32[1024]{0:T(1024)S(1)} %pad_clamp_fusion), kind=kCustom, calls=%fused_computation.1 | custom fusion | bytes 1573888 | tf_op jit(solution)/shard_map/jit(_take)/gather | solution.py:71
  43.6 1.5 fusion.6
  45.1 1.1 broadcast_select_fusion.1
  46.2 1.5 broadcast_select_fusion.2
  47.7 1.5 broadcast_select_fusion.3
  49.2 1.5 broadcast_select_fusion.4
  50.7 1.5 broadcast_select_fusion.5
  52.2 1.5 broadcast_select_fusion.6
  53.7 1.5 broadcast_select_fusion.7
  55.3 1.7 %fusion.7 = (bf16[2,256,513]{2,0,1:T(2,128)(2,1)S(1)}, bf16[2,256,513]{2,0,1:T(2,128)(2,1)S(1)}) fusion(bf16[2,256,514]{2,0,1:T(2,128)(2,1)S(1)} %broadcast_select_fusion.7), kind=kLoop, calls=%fused_computation.45 | loop fusion | bytes 2101248 | tf_op jit(solution)/shard_map/slice | solution.py:53
  57.0 2.7 %multiply_reduce_fusion.2 = f32[256,512]{1,0:T(8,128)} fusion(f32[2]{0:T(128)S(1)} %convert_multiply_fusion, pred[2,256]{0,1:T(8,128)(4,1)S(1)} %copy.29, bf16[2,256,513]{2,0,1:T(2,128)(2,1)S(1)} %get-tuple-element.39, bf16[2,256,513]{2,0,1:T(2,128)(2,1)S(1)} %get-tuple-element.38), kind=kLoop, calls=%fused_computation.26 | loop fusion | flops 917504 | bytes 1573384 | tf_op jit(solution)/shard_map/reduce_sum | solution.py:75
  59.6 96.7 %all-gather.3.cloned.1.call-done = f32[2048,512]{1,0:T(8,128)} async-done(((f32[256,512]{1,0:T(8,128)}), f32[2048,512]{1,0:T(8,128)}) %all-gather.3.cloned.1.call-update) | async-done | bytes 4194320 | tf_op jit(solution)/shard_map/all_gather | solution.py:75
  156.3 2.7 %reduce_sum.37 = f32[256,512]{1,0:T(8,128)S(1)} reduce(f32[8,256,512]{2,1,0:T(8,128)} %bitcast.58, f32[]{:T(128)} %constant.84.clone.1), dimensions={0}, to_apply=%region_7.8 | reduce | flops 917504 | bytes 4718596 | tf_op jit(solution)/shard_map/reduce_sum | solution.py:74
  (60 shorter events, 7.7 us)
Async XLA Ops:
  6.5 149.8 %all-gather.3.cloned.1.call-start = ((), (), s32[]{:S(2)}) async-start(), calls=%async_computation | async-start | bytes 4718592 | tf_op jit(solution)/shard_map/all_gather | solution.py:75
  7.2 7.1 %collective-permute-start = (bf16[2,3,256]{2,1,0:T(4,128)(2,1)S(1)}, bf16[2,3,256]{2,1,0:T(4,128)(2,1)S(1)}, u32[]{:S(2)}, u32[]{:S(2)}) collective-permute-start(bf16[2,3,256]{2,1,0:T(4,128)(2,1)S(1)} %slice.101), channel_id=1, source_target_pairs={{1,0},{2,1},{3,2},{4,3},{5,4},{6,5},{7,6},{8,7},{9,8},{10,9},{11,1... | collective-permute-start | bytes 9224 | tf_op jit(solution)/shard_map/ppermute | solution.py:15
  17.5 2.9 %copy-start = (bf16[2,256,768]{2,1,0:T(8,128)(2,1)S(1)}, bf16[2,256,768]{2,1,0:T(8,128)(2,1)}, u32[]{:S(2)}) copy-start(bf16[2,256,768]{2,1,0:T(8,128)(2,1)} %get-tuple-element.93) | copy-start | bytes 2359300 | tf_op jit(solution)/shard_map/while
  20.3 1.0 copy-start.1
  21.7 0.8 copy-start.2
  25.6 2.9 %copy-start = (bf16[2,256,768]{2,1,0:T(8,128)(2,1)S(1)}, bf16[2,256,768]{2,1,0:T(8,128)(2,1)}, u32[]{:S(2)}) copy-start(bf16[2,256,768]{2,1,0:T(8,128)(2,1)} %get-tuple-element.93) | copy-start | bytes 2359300 | tf_op jit(solution)/shard_map/while
  28.4 1.0 copy-start.1
  29.9 0.8 copy-start.2
  30.7 7.6 %copy-start.3 = (s32[2]{0:T(128)S(1)}, s32[2]{0:T(128)}, u32[]{:S(2)}) copy-start(s32[2]{0:T(128)} %param.10) | copy-start | bytes 28
  32.4 8.2 %collective-permute-start.1 = (bf16[2,256,256]{2,0,1:T(2,128)(2,1)S(1)}, bf16[2,256,256]{2,0,1:T(2,128)(2,1)S(1)}, u32[]{:S(2)}, u32[]{:S(2)}) collective-permute-start(bf16[2,256,256]{2,0,1:T(2,128)(2,1)S(1)} %slice.102), channel_id=1, source_target_pairs={{1,0},{2,1},{3,2},{4,3},{5,4},{6,5},{7,6},{8,7},{9,8},{10,9},{11,1... | collective-permute-start | bytes 786440 | tf_op jit(solution)/shard_map/ppermute | solution.py:15
Sparse Core Ops, SparseCore 0:
  59.8 96.4 all-gather.2
